TPU v7x, 32 devices: a whole 2x2x4 slice. The times are simulated.
32 devices in a mesh: row: 4 (over y, x), col: 8 (over z, core).
Axes of the slice: x: 2, y: 2, z: 4, core: 2. Of those that a mesh axis runs over, the one named last changes fastest.
Arguments:
- teacher: bfloat16 [16384, 256], replicated, may hold values from -4 to 4
- panel_ids: int32 [2048], P('col'), may hold values from 0 to 16383
- rest_ids: int32 [4, 8, 128], P('row', 'col'), may hold values from 0 to 16383
- inverse: bfloat16 [2048, 2048], replicated, may hold values from -1 to 1, as said below
Outputs:
- trailing: float32 [8, 4, 128, 4, 8, 128], P(None, 'row', None, None, 'col')
- panel_rows: bfloat16 [4, 8, 128, 2048], P('row', 'col')
Inputs may be any that keep to these rules, and one draw needn't show every extreme that they name: `inverse`: zero above the diagonal.
All inputs are finite; a program needn't handle non-finite values.
Results may differ from a plain program's by a relative error of at most 0.0049.
Values may be sent and summed in bfloat16 or wider, within the bound.
A program may use at most 128 MiB of HBM per device.

v0:
```python
import jax
import jax.numpy as jnp
from jax import lax
from jax.sharding import PartitionSpec as P


def gaussian(left_rows, right_rows, inv_scale):
    sq_left = jnp.sum(jnp.square(left_rows.astype(jnp.float32)), axis=-1)
    sq_right = jnp.sum(jnp.square(right_rows.astype(jnp.float32)), axis=-1)
    inner = lax.dot_general(
        left_rows, right_rows, (((1,), (1,)), ((), ())), preferred_element_type=jnp.float32
    )
    return jnp.exp(-inv_scale * (sq_left[:, None] + sq_right[None, :] - 2.0 * inner))


def factor(rows_emb, panel_emb, inverse, inv_scale):
    kernel = gaussian(rows_emb, panel_emb, inv_scale).astype(jnp.bfloat16)
    block_width = inverse.shape[0] // 4
    pieces = []
    for block_at in range(4):
        finish = (block_at + 1) * block_width
        pieces.append(
            lax.dot_general(
                kernel[:, :finish],
                inverse[block_at * block_width : finish, :finish],
                (((1,), (1,)), ((), ())),
                preferred_element_type=jnp.float32,
            )
        )
    return jnp.concatenate(pieces, 1).astype(jnp.bfloat16)


def shards(teacher, panel_ids, rest_ids, inverse):
    n_row = lax.axis_size("row")
    n_col = lax.axis_size("col")
    row_at = lax.axis_index("row")
    col_at = lax.axis_index("col")
    stretch_rows = rest_ids.shape[2]
    inv_scale = 2.0 / teacher.shape[1]
    gathered = lax.all_gather(rest_ids, ("row", "col"), axis=0, tiled=True)
    blocks = gathered.reshape(n_row * n_col, stretch_rows)
    panel = lax.all_gather(panel_ids, "col", axis=0, tiled=True)
    panel_emb = teacher[panel]
    own_ids = lax.dynamic_slice_in_dim(blocks, row_at * n_col + col_at, 1, 0).reshape(stretch_rows)
    col_ids = lax.dynamic_slice_in_dim(
        blocks.reshape(n_row, n_col, stretch_rows), col_at, 1, 1
    ).reshape(-1)
    row_ids = lax.dynamic_slice_in_dim(
        blocks.reshape(n_col, n_row, stretch_rows), row_at, 1, 1
    ).reshape(-1)
    own_factor = factor(teacher[own_ids], panel_emb, inverse, inv_scale)
    col_emb = teacher[col_ids]
    col_factor = lax.all_gather(own_factor, "row", axis=0, tiled=True)
    row_emb = teacher[row_ids]
    kernel = gaussian(row_emb, col_emb, inv_scale)
    row_factor = factor(row_emb, panel_emb, inverse, inv_scale)
    update = lax.dot_general(
        row_factor, col_factor, (((1,), (1,)), ((), ())), preferred_element_type=jnp.float32
    )
    rows_local = jnp.arange(n_col * stretch_rows, dtype=jnp.int32)
    row_index = (
        rows_local // stretch_rows * n_row + row_at
    ) * stretch_rows + rows_local % stretch_rows
    cols_local = jnp.arange(n_row * stretch_rows, dtype=jnp.int32)
    col_index = (
        cols_local // stretch_rows * n_col + col_at
    ) * stretch_rows + cols_local % stretch_rows
    result = kernel - update
    trailing = jnp.where(row_index[:, None] >= col_index[None, :], result, jnp.zeros_like(result))
    return (
        trailing.reshape(n_col, 1, stretch_rows, n_row, 1, stretch_rows),
        own_factor.reshape(1, 1, stretch_rows, own_factor.shape[1]),
    )


def solution(mesh):
    return jax.shard_map(
        shards,
        mesh=mesh,
        in_specs=(P(), P("col"), P("row", "col", None), P()),
        out_specs=(P(None, "row", None, None, "col", None), P("row", "col", None, None)),
        check_vma=False,
    )
```

profile of v0, /device:TPU:0, one launch (start us, length us, event | category | flops | bytes accessed | tf_op | source)
XLA Modules:
  0.0 132.2 jit_solution(9935352924947401463)
XLA Ops:
  7.2 0.0 all-gather.3.cloned.1.call-start
  7.2 43.5 %all_gather.9 = s32[32,1,128]{2,1,0:T(1,128)S(1)} all-gather(s32[1,1,128]{2,1,0:T(1,128)} %param.6), channel_id=1, replica_groups=mesh['row'=4,'col'=8] {'row','col'}, dimensions={0}, use_global_device_ids=true | all-gather | bytes 16896 | tf_op jit(solution)/shard_map/all_gather | solution.py:40
  50.7 5.2 %gather_fusion.3 = bf16[128,256]{1,0:T(8,128)(2,1)S(1)} fusion(bf16[16384,256]{1,0:T(8,128)(2,1)} %param.4, s32[1024]{0:T(1024)S(1)} %pad_clamp_fusion), kind=kCustom, calls=%fused_computation.3 | custom fusion | bytes 131584 | tf_op jit(solution)/shard_map/gather | solution.py:51
  55.9 0.1 multiply_reduce_fusion.3
  56.0 9.0 %all-gather = s32[8,1,256]{2,1,0:T(1,128)S(1)} all-gather(s32[1,1,256]{2,1,0:T(1,128)} %bitcast.42), channel_id=1, replica_groups=mesh['row'=4,'col'=8] {'col'}, dimensions={0}, use_global_device_ids=true | all-gather | bytes 9216 | tf_op jit(solution)/shard_map/all_gather | solution.py:42
  65.0 11.1 %gather_fusion.2 = bf16[2048,256]{1,0:T(8,128)(2,1)S(1)} fusion(bf16[16384,256]{1,0:T(8,128)(2,1)} %param.4, s32[2048]{0:T(1024)S(1)} %fusion.46), kind=kCustom, calls=%fused_computation.2 | custom fusion | bytes 2105344 | tf_op jit(solution)/shard_map/gather | solution.py:43
  76.1 0.3 multiply_reduce_fusion
  76.5 0.5 fusion.13
  77.0 1.3 %convolution_convert_fusion.1 = bf16[128,512]{1,0:T(8,128)(2,1)S(1)} fusion(bf16[2048,2048]{1,0:T(8,128)(2,1)} %param.7, bf16[128,2048]{1,0:T(8,128)(2,1)S(1)} %fusion.13), kind=kOutput, calls=%fused_computation.36 | convolution fusion | flops 67174400 | bytes 786432 | tf_op jit(solution)/shard_map/dot_general | solution.py:23
  78.4 1.7 %convolution_convert_fusion.2 = bf16[128,512]{1,0:T(8,128)(2,1)S(1)} fusion(bf16[2048,2048]{1,0:T(8,128)(2,1)} %param.7, bf16[128,2048]{1,0:T(8,128)(2,1)S(1)} %fusion.13), kind=kOutput, calls=%fused_computation.37 | convolution fusion | flops 134283264 | bytes 1441792 | tf_op jit(solution)/shard_map/dot_general | solution.py:23
  80.1 2.4 %fusion.32 = bf16[128,512]{1,0:T(8,128)(2,1)S(1)} fusion(bf16[128,2048]{1,0:T(8,128)(2,1)S(1)} %fusion.13, bf16[2048,2048]{1,0:T(8,128)(2,1)} %param.7), kind=kOutput, calls=%fused_computation.35 | convolution fusion | flops 268500992 | bytes 2752512 | tf_op jit(solution)/shard_map/dot_general | solution.py:23
  82.5 2.1 %fusion.35 = bf16[128,512]{1,0:T(8,128)(2,1)S(1)} fusion(bf16[2048,2048]{1,0:T(8,128)(2,1)} %param.7, bf16[128,2048]{1,0:T(8,128)(2,1)S(1)} %fusion.13), kind=kOutput, calls=%fused_computation.38 | convolution fusion | flops 201392128 | bytes 2097152 | tf_op jit(solution)/shard_map/dot_general | solution.py:23
  84.6 0.8 pad_maximum_fusion
  85.4 0.0 all-gather.3.cloned.1.call-update
  85.5 7.9 %gather_fusion = bf16[1024,256]{1,0:T(8,128)(2,1)S(1)} fusion(bf16[16384,256]{1,0:T(8,128)(2,1)} %param.4, s32[1024]{0:T(1024)S(1)} %broadcast_clamp_fusion), kind=kCustom, calls=%fused_computation | custom fusion | bytes 1052672 | tf_op jit(solution)/shard_map/gather | solution.py:54
  93.4 6.0 %gather_fusion.1 = bf16[512,256]{1,0:T(8,128)(2,1)S(1)} fusion(bf16[16384,256]{1,0:T(8,128)(2,1)} %param.4, s32[1024]{0:T(1024)S(1)} %pad_clamp_fusion.1), kind=kCustom, calls=%fused_computation.1 | custom fusion | bytes 526336 | tf_op jit(solution)/shard_map/gather | solution.py:52
  99.5 0.1 multiply_reduce_fusion.2
  99.7 0.2 multiply_reduce_fusion.1
  99.9 0.0 slice-start
  99.9 0.8 pad_maximum_fusion.1
  100.7 0.0 slice-start.1
  100.7 2.6 %exponential_convert_fusion = bf16[1024,2048]{1,0:T(8,128)(2,1)S(1)} fusion(bf16[1024,256]{1,0:T(8,128)(2,1)S(1)} %gather_fusion, bf16[2048,256]{1,0:T(8,128)(2,1)S(1)} %gather_fusion.2, f32[2048]{0:T(1024)S(1)} %multiply_reduce_fusion, f32[1024]{0:T(1024)S(1)} %multiply_reduce_fusion.1), kind=kOutput, calls=%fused_computation.4 | convolution fusion | flops 1084227584 | bytes 5779456 | tf_op jit(solution)/shard_map/dot_general | solution.py:10
  103.3 0.0 slice-done
  103.3 0.4 slice-done.1
  103.7 0.7 convolution_convert_fusion
  104.4 1.3 fusion.20
  105.7 2.8 %fusion.23 = bf16[1024,512]{1,0:T(8,128)(2,1)} fusion(bf16[1024,2048]{1,0:T(8,128)(2,1)S(1)} %exponential_convert_fusion, bf16[2048,2048]{1,0:T(8,128)(2,1)S(1)} %bitcast.44), kind=kOutput, calls=%fused_computation.29 | convolution fusion | flops 1611137024 | bytes 5767168 | tf_op jit(solution)/shard_map/dot_general | solution.py:23
  108.5 3.3 %fusion.26 = bf16[1024,512]{1,0:T(8,128)(2,1)} fusion(bf16[1024,2048]{1,0:T(8,128)(2,1)S(1)} %exponential_convert_fusion, bf16[2048,2048]{1,0:T(8,128)(2,1)S(1)} %bitcast.44), kind=kOutput, calls=%fused_computation.31 | convolution fusion | flops 2148007936 | bytes 7340032 | tf_op jit(solution)/shard_map/dot_general | solution.py:23
  111.9 6.3 %all-gather.3.cloned.1.call-done = bf16[512,2048]{1,0:T(8,128)(2,1)} async-done(((bf16[128,2048]{1,0:T(8,128)(2,1)}), bf16[512,2048]{1,0:T(8,128)(2,1)}) %all-gather.3.cloned.1.call-update) | async-done | bytes 2097168 | tf_op jit(solution)/shard_map/all_gather | solution.py:53
  118.2 4.5 %fusion = f32[1024,512]{1,0:T(8,128)S(1)} fusion(bf16[512,2048]{1,0:T(8,128)(2,1)} %all-gather.3.cloned.1.call-done, bf16[1024,512]{1,0:T(8,128)(2,1)} %fusion.26, bf16[1024,512]{1,0:T(8,128)(2,1)} %fusion.23, bf16[1024,512]{1,0:T(8,128)(2,1)S(1)} %fusion.20, bf16[1024,512]{1,0:T(8,128)(2,1)S(1)} %convolution_convert_fusion), kind=kOutput, calls=%fused_computation.5 | convolution fusion | flops 2164260864 | bytes 8388608 | tf_op jit(solution)/shard_map/dot_general | solution.py:57
  122.8 0.8 subtract_select_fusion
  123.6 1.7 %reshape.218 = f32[8,1,128,4,1,128]{5,3,2,0,4,1:T(4,128)} reshape(f32[1024,512]{1,0:T(8,128)S(1)} %subtract_select_fusion) | data formatting | bytes 4194304 | tf_op jit(solution)/shard_map/reshape | solution.py:71
  (10 shorter events, 0.1 us)
Async XLA Ops:
  7.2 111.1 %all-gather.3.cloned.1.call-start = ((), (), s32[]{:S(2)}) async-start(), calls=%async_computation | async-start | bytes 2621440 | tf_op jit(solution)/shard_map/all_gather | solution.py:53
  99.9 3.4 %slice-start = ((s8[8388608]{0:T(1024)(128)(4,1)}), s8[4194304]{0:T(1024)(128)(4,1)S(1)}, s32[]{:S(2)}) async-start(s8[8388608]{0:T(1024)(128)(4,1)} %bitcast.43), calls=%async_computation.1 | async-start | bytes 8388608
  100.7 3.0 %slice-start.1 = ((s8[8388608]{0:T(1024)(128)(4,1)}), s8[4194304]{0:T(1024)(128)(4,1)S(1)}, s32[]{:S(2)}) async-start(s8[8388608]{0:T(1024)(128)(4,1)} %bitcast.43), calls=%async_computation.2 | async-start | bytes 8388608
Sparse Core Ops, SparseCore 0:
  85.6 32.6 all-gather.2
where the time goes:
time: 133 us; the launch traced here: 132 us
  blocking collectives  52.5 us (39%)
  local copies, waits for them, and re-layouts  32.4 us (24%)
  matrix products  24.1 us (18%)
  between operations  14.2 us (11%)
  waiting for transfers between devices  6.36 us (5%)
  other arithmetic  2.57 us (2%)
    all_gather x1, blocking collectives, shards(): gathered = lax.all_gather(rest_ids, ('row', 'col'), axis=0, tiled=True)  43.5 us
    dot_general x8, matrix products, factor(): lax.dot_general(kernel[:, :finish], inverse[block_at * block_width:finish...  15.7 us
    gather x1, local copies, waits for them, and re-layouts, shards(): panel_emb = teacher[panel]  11.1 us
    all_gather x1, blocking collectives, shards(): panel = lax.all_gather(panel_ids, 'col', axis=0, tiled=True)  8.99 us
    gather x1, local copies, waits for them, and re-layouts, shards(): row_emb = teacher[row_ids]  7.92 us
    all_gather x1, waiting for transfers between devices, shards(): col_factor = lax.all_gather(own_factor, 'row', axis=0, tiled=True)  6.34 us
    gather x1, local copies, waits for them, and re-layouts, shards(): col_emb = teacher[col_ids]  6.02 us
    gather x1, local copies, waits for them, and re-layouts, shards(): own_factor = factor(teacher[own_ids], panel_emb, inverse, inv_scale)  5.22 us
  transfers between devices with their start and end apart: 1, of which 1 were waited for; matrix products, arithmetic and copies ran while one was open for 20% of the time, Pallas kernels for 0%

commit v1 on v0

--- a/solution.py
+++ b/solution.py
@@ -2,6 +2,19 @@
 import jax.numpy as jnp
 from jax import lax
 from jax.sharding import PartitionSpec as P
+
+
+def ring_gather(x, axis, dim):
+    ways = lax.axis_size(axis)
+    up = [(d, (d + 1) % ways) for d in range(ways)]
+    down = [(d, (d - 1) % ways) for d in range(ways)]
+    earlier, later = ([x], [x])
+    for _ in range(ways // 2):
+        earlier.append(lax.ppermute(earlier[-1], axis, up))
+    for _ in range((ways - 1) // 2):
+        later.append(lax.ppermute(later[-1], axis, down))
+    line = jnp.concatenate([*earlier[::-1], *later[1:]], axis=dim)
+    return jnp.roll(line, (lax.axis_index(axis) - ways // 2) * x.shape[dim], axis=dim)
 
 
 def gaussian(left_rows, right_rows, inv_scale):
@@ -39,7 +52,7 @@
     inv_scale = 2.0 / teacher.shape[1]
     gathered = lax.all_gather(rest_ids, ("row", "col"), axis=0, tiled=True)
     blocks = gathered.reshape(n_row * n_col, stretch_rows)
-    panel = lax.all_gather(panel_ids, "col", axis=0, tiled=True)
+    panel = ring_gather(panel_ids, "col", 0)
     panel_emb = teacher[panel]
     own_ids = lax.dynamic_slice_in_dim(blocks, row_at * n_col + col_at, 1, 0).reshape(stretch_rows)
     col_ids = lax.dynamic_slice_in_dim(

time: 133 us -> 150 us (1.13)
  waiting for transfers between devices: 6.36 us -> 22.8 us
  starting transfers between devices: 0.04 us -> 12.2 us
  blocking collectives: 52.5 us -> 40.6 us
    ppermute x0 -> x7, starting transfers between devices: none -> 12.2 us  [the longest x3 11.3 us: ring_gather(): later.append(lax.ppermute(later[-1], axis, down))]
    all_gather x1, waiting for transfers between devices: 6.34 us -> 16 us  [shards(): col_factor = lax.all_gather(own_factor, 'row', axis=0, tiled=True)]
    all_gather x1 -> x0, blocking collectives: 8.99 us -> none  [shards(): panel = lax.all_gather(panel_ids, 'col', axis=0, tiled=True)]
    ppermute x0 -> x7, waiting for transfers between devices: none -> 6.75 us  [the longest x4 5.54 us: ring_gather(): earlier.append(lax.ppermute(earlier[-1], axis, up))]
    all_gather x1, blocking collectives: 43.5 us -> 40.6 us  [shards(): gathered = lax.all_gather(rest_ids, ('row', 'col'), axis=0, tiled=True)]
  transfers between devices with their start and end apart: 1 -> 8, of which waited for: 1 -> 4; matrix products, arithmetic and copies ran while one was open for 20% -> 21% of each run, Pallas kernels for 0% -> 0%
where the time goes in v1:
time: 150 us
  blocking collectives  40.6 us (27%)
  local copies, waits for them, and re-layouts  33 us (22%)
  matrix products  24 us (16%)
  waiting for transfers between devices  22.8 us (15%)
  between operations  14.4 us (10%)
  starting transfers between devices  12.2 us (8%)
  other arithmetic  2.64 us (2%)
    all_gather x1, blocking collectives, shards(): gathered = lax.all_gather(rest_ids, ('row', 'col'), axis=0, tiled=True)  40.6 us
    all_gather x1, waiting for transfers between devices, shards(): col_factor = lax.all_gather(own_factor, 'row', axis=0, tiled=True)  16 us
    dot_general x8, matrix products, factor(): lax.dot_general(kernel[:, :finish], inverse[block_at * block_width:finish...  15.7 us
    gather x1, local copies, waits for them, and re-layouts, shards(): panel_emb = teacher[panel]  11.3 us
    ppermute x3, starting transfers between devices, ring_gather(): later.append(lax.ppermute(later[-1], axis, down))  11.3 us
    gather x1, local copies, waits for them, and re-layouts, shards(): row_emb = teacher[row_ids]  7.92 us
    gather x1, local copies, waits for them, and re-layouts, shards(): col_emb = teacher[col_ids]  6.02 us
    ppermute x4, waiting for transfers between devices, ring_gather(): earlier.append(lax.ppermute(earlier[-1], axis, up))  5.54 us
  transfers between devices with their start and end apart: 8, of which 4 were waited for; matrix products, arithmetic and copies ran while one was open for 21% of the time, Pallas kernels for 0%

profile of v1, /device:TPU:0, one launch (start us, length us, event | category | flops | bytes accessed | tf_op | source)
XLA Modules:
  0.0 149.6 jit_solution(6067839753580586553)
XLA Ops:
  7.2 0.0 copy-start
  7.2 0.0 all-gather.2.cloned.1.call-start
  7.2 0.5 collective-permute-start
  7.8 4.1 %collective-permute-start.4 = (s32[256]{0:T(256)}, s32[256]{0:T(256)S(1)}, u32[]{:S(2)}, u32[]{:S(2)}) collective-permute-start(s32[256]{0:T(256)} %param.5), channel_id=1, source_target_pairs={{0,7},{1,0},{2,1},{3,2},{4,3},{5,4},{6,5},{7,6},{8,15},{9,8},{10,9... | collective-permute-start | bytes 3080 | tf_op jit(solution)/shard_map/ppermute | solution.py:15
  11.9 40.6 %all_gather.6 = s32[32,1,128]{2,1,0:T(1,128)S(1)} all-gather(s32[1,1,128]{2,1,0:T(1,128)} %param.6), channel_id=1, replica_groups=mesh['row'=4,'col'=8] {'row','col'}, dimensions={0}, use_global_device_ids=true | all-gather | bytes 16896 | tf_op jit(solution)/shard_map/all_gather | solution.py:53
  52.5 5.2 %gather_fusion.3 = bf16[128,256]{1,0:T(8,128)(2,1)S(1)} fusion(bf16[16384,256]{1,0:T(8,128)(2,1)} %param.4, s32[1024]{0:T(1024)S(1)} %pad_clamp_fusion), kind=kCustom, calls=%fused_computation.3 | custom fusion | bytes 131584 | tf_op jit(solution)/shard_map/gather | solution.py:64
  57.8 0.0 collective-permute-done
  57.8 0.4 collective-permute-start.1
  58.2 0.1 multiply_reduce_fusion.3
  58.3 4.3 %collective-permute-done.1 = s32[256]{0:T(256)S(1)} collective-permute-done((s32[256]{0:T(256)S(1)}, s32[256]{0:T(256)S(1)}, u32[]{:S(2)}, u32[]{:S(2)}) %collective-permute-start.1) | collective-permute-done | bytes 1056 | tf_op jit(solution)/shard_map/ppermute | solution.py:13
  62.6 0.0 collective-permute-start.2
  62.6 0.0 collective-permute-done.4
  62.6 3.6 %collective-permute-start.5 = (s32[256]{0:T(256)S(1)}, s32[256]{0:T(256)S(1)}, u32[]{:S(2)}, u32[]{:S(2)}) collective-permute-start(s32[256]{0:T(256)S(1)} %collective-permute-done.4), channel_id=1, source_target_pairs={{0,7},{1,0},{2,1},{3,2},{4,3},{5,4},{6,5},{7,6},{8,15},{9,8},{10,9... | collective-permute-start | bytes 3080 | tf_op jit(solution)/shard_map/ppermute | solution.py:15
  66.2 1.2 collective-permute-done.2
  67.4 0.0 collective-permute-start.3
  67.4 7.9 %gather_fusion = bf16[1024,256]{1,0:T(8,128)(2,1)S(1)} fusion(bf16[16384,256]{1,0:T(8,128)(2,1)} %param.4, s32[1024]{0:T(1024)S(1)} %broadcast_clamp_fusion), kind=kCustom, calls=%fused_computation | custom fusion | bytes 1052672 | tf_op jit(solution)/shard_map/gather | solution.py:67
  75.4 0.0 collective-permute-done.5
  75.4 3.6 %collective-permute-start.6 = (s32[256]{0:T(256)S(1)}, s32[256]{0:T(256)S(1)}, u32[]{:S(2)}, u32[]{:S(2)}) collective-permute-start(s32[256]{0:T(256)S(1)} %collective-permute-done.5), channel_id=1, source_target_pairs={{0,7},{1,0},{2,1},{3,2},{4,3},{5,4},{6,5},{7,6},{8,15},{9,8},{10,9... | collective-permute-start | bytes 3080 | tf_op jit(solution)/shard_map/ppermute | solution.py:15
  79.0 0.0 collective-permute-done.3
  79.0 0.0 copy-done
  79.1 1.2 collective-permute-done.6
  80.4 0.1 fusion.46
  80.4 11.3 %gather_fusion.2 = bf16[2048,256]{1,0:T(8,128)(2,1)S(1)} fusion(bf16[16384,256]{1,0:T(8,128)(2,1)} %param.4, s32[2048]{0:T(1024)S(1)} %fusion.46), kind=kCustom, calls=%fused_computation.2 | custom fusion | bytes 2105344 | tf_op jit(solution)/shard_map/gather | solution.py:56
  91.7 0.3 multiply_reduce_fusion
  92.1 0.5 fusion.13
  92.6 1.3 convolution_convert_fusion.1
  94.0 1.7 %convolution_convert_fusion.2 = bf16[128,512]{1,0:T(8,128)(2,1)S(1)} fusion(bf16[2048,2048]{1,0:T(8,128)(2,1)} %param.7, bf16[128,2048]{1,0:T(8,128)(2,1)S(1)} %fusion.13), kind=kOutput, calls=%fused_computation.37 | convolution fusion | flops 134283264 | bytes 1441792 | tf_op jit(solution)/shard_map/dot_general | solution.py:36
  95.7 2.4 %fusion.32 = bf16[128,512]{1,0:T(8,128)(2,1)S(1)} fusion(bf16[128,2048]{1,0:T(8,128)(2,1)S(1)} %fusion.13, bf16[2048,2048]{1,0:T(8,128)(2,1)} %param.7), kind=kOutput, calls=%fused_computation.35 | convolution fusion | flops 268500992 | bytes 2752512 | tf_op jit(solution)/shard_map/dot_general | solution.py:36
  98.1 2.1 %fusion.35 = bf16[128,512]{1,0:T(8,128)(2,1)S(1)} fusion(bf16[2048,2048]{1,0:T(8,128)(2,1)} %param.7, bf16[128,2048]{1,0:T(8,128)(2,1)S(1)} %fusion.13), kind=kOutput, calls=%fused_computation.38 | convolution fusion | flops 201392128 | bytes 2097152 | tf_op jit(solution)/shard_map/dot_general | solution.py:36
  100.2 0.8 pad_maximum_fusion
  101.0 0.0 all-gather.2.cloned.1.call-update
  101.0 6.0 %gather_fusion.1 = bf16[512,256]{1,0:T(8,128)(2,1)S(1)} fusion(bf16[16384,256]{1,0:T(8,128)(2,1)} %param.4, s32[1024]{0:T(1024)S(1)} %pad_clamp_fusion.1), kind=kCustom, calls=%fused_computation.1 | custom fusion | bytes 526336 | tf_op jit(solution)/shard_map/gather | solution.py:65
  107.1 0.1 multiply_reduce_fusion.2
  107.3 0.2 multiply_reduce_fusion.1
  107.5 0.0 slice-start
  107.5 0.8 pad_maximum_fusion.1
  108.3 0.0 slice-start.1
  108.3 2.4 %exponential_convert_fusion = bf16[1024,2048]{1,0:T(8,128)(2,1)S(1)} fusion(bf16[1024,256]{1,0:T(8,128)(2,1)S(1)} %gather_fusion, bf16[2048,256]{1,0:T(8,128)(2,1)S(1)} %gather_fusion.2, f32[2048]{0:T(1024)S(1)} %multiply_reduce_fusion, f32[1024]{0:T(1024)S(1)} %multiply_reduce_fusion.1), kind=kOutput, calls=%fused_computation.4 | convolution fusion | flops 1084227584 | bytes 5779456 | tf_op jit(solution)/shard_map/dot_general | solution.py:23
  110.7 0.0 slice-done
  110.7 0.7 slice-done.1
  111.5 0.7 convolution_convert_fusion
  112.2 1.3 fusion.20
  113.5 2.8 %fusion.23 = bf16[1024,512]{1,0:T(8,128)(2,1)} fusion(bf16[1024,2048]{1,0:T(8,128)(2,1)S(1)} %exponential_convert_fusion, bf16[2048,2048]{1,0:T(8,128)(2,1)S(1)} %bitcast.40), kind=kOutput, calls=%fused_computation.29 | convolution fusion | flops 1611137024 | bytes 5767168 | tf_op jit(solution)/shard_map/dot_general | solution.py:36
  116.3 3.3 %fusion.26 = bf16[1024,512]{1,0:T(8,128)(2,1)} fusion(bf16[1024,2048]{1,0:T(8,128)(2,1)S(1)} %exponential_convert_fusion, bf16[2048,2048]{1,0:T(8,128)(2,1)S(1)} %bitcast.40), kind=kOutput, calls=%fused_computation.31 | convolution fusion | flops 2148007936 | bytes 7340032 | tf_op jit(solution)/shard_map/dot_general | solution.py:36
  119.6 16.0 %all-gather.2.cloned.1.call-done = bf16[512,2048]{1,0:T(8,128)(2,1)} async-done(((bf16[128,2048]{1,0:T(8,128)(2,1)}), bf16[512,2048]{1,0:T(8,128)(2,1)}) %all-gather.2.cloned.1.call-update) | async-done | bytes 2097168 | tf_op jit(solution)/shard_map/all_gather | solution.py:66
  135.7 4.5 %fusion = f32[1024,512]{1,0:T(8,128)S(1)} fusion(bf16[512,2048]{1,0:T(8,128)(2,1)} %all-gather.2.cloned.1.call-done, bf16[1024,512]{1,0:T(8,128)(2,1)} %fusion.26, bf16[1024,512]{1,0:T(8,128)(2,1)} %fusion.23, bf16[1024,512]{1,0:T(8,128)(2,1)S(1)} %fusion.20, bf16[1024,512]{1,0:T(8,128)(2,1)S(1)} %convolution_convert_fusion), kind=kOutput, calls=%fused_computation.5 | convolution fusion | flops 2164260864 | bytes 8388608 | tf_op jit(solution)/shard_map/dot_general | solution.py:70
  140.2 0.8 subtract_select_fusion
  141.0 1.7 %reshape.218 = f32[8,1,128,4,1,128]{5,3,2,0,4,1:T(4,128)} reshape(f32[1024,512]{1,0:T(8,128)S(1)} %subtract_select_fusion) | data formatting | bytes 4194304 | tf_op jit(solution)/shard_map/reshape | solution.py:84
  (26 shorter events, 0.2 us)
Async XLA Ops:
  7.2 71.8 %copy-start = (s32[256]{0:T(256)S(1)}, s32[256]{0:T(256)}, u32[]{:S(2)}) copy-start(s32[256]{0:T(256)} %param.5) | copy-start | bytes 3076
  7.2 128.5 %all-gather.2.cloned.1.call-start = ((), (), s32[]{:S(2)}) async-start(), calls=%async_computation | async-start | bytes 2621440 | tf_op jit(solution)/shard_map/all_gather | solution.py:66
  7.2 50.5 %collective-permute-start = (s32[256]{0:T(256)}, s32[256]{0:T(256)S(1)}, u32[]{:S(2)}, u32[]{:S(2)}) collective-permute-start(s32[256]{0:T(256)} %param.5), channel_id=1, source_target_pairs={{0,1},{1,2},{2,3},{3,4},{4,5},{5,6},{6,7},{7,0},{8,9},{9,10},{10,1... | collective-permute-start | bytes 3080 | tf_op jit(solution)/shard_map/ppermute | solution.py:13
  7.8 54.9 %collective-permute-start.4 = (s32[256]{0:T(256)}, s32[256]{0:T(256)S(1)}, u32[]{:S(2)}, u32[]{:S(2)}) collective-permute-start(s32[256]{0:T(256)} %param.5), channel_id=1, source_target_pairs={{0,7},{1,0},{2,1},{3,2},{4,3},{5,4},{6,5},{7,6},{8,15},{9,8},{10,9... | collective-permute-start | bytes 3080 | tf_op jit(solution)/shard_map/ppermute | solution.py:15
  57.8 4.8 %collective-permute-start.1 = (s32[256]{0:T(256)S(1)}, s32[256]{0:T(256)S(1)}, u32[]{:S(2)}, u32[]{:S(2)}) collective-permute-start(s32[256]{0:T(256)S(1)} %collective-permute-done), channel_id=1, source_target_pairs={{0,1},{1,2},{2,3},{3,4},{4,5},{5,6},{6,7},{7,0},{8,9},{9,10},{10,1... | collective-permute-start | bytes 3080 | tf_op jit(solution)/shard_map/ppermute | solution.py:13
  62.6 4.8 %collective-permute-start.2 = (s32[256]{0:T(256)S(1)}, s32[256]{0:T(256)S(1)}, u32[]{:S(2)}, u32[]{:S(2)}) collective-permute-start(s32[256]{0:T(256)S(1)} %collective-permute-done.1), channel_id=1, source_target_pairs={{0,1},{1,2},{2,3},{3,4},{4,5},{5,6},{6,7},{7,0},{8,9},{9,10},{10,1... | collective-permute-start | bytes 3080 | tf_op jit(solution)/shard_map/ppermute | solution.py:13
  62.6 12.7 %collective-permute-start.5 = (s32[256]{0:T(256)S(1)}, s32[256]{0:T(256)S(1)}, u32[]{:S(2)}, u32[]{:S(2)}) collective-permute-start(s32[256]{0:T(256)S(1)} %collective-permute-done.4), channel_id=1, source_target_pairs={{0,7},{1,0},{2,1},{3,2},{4,3},{5,4},{6,5},{7,6},{8,15},{9,8},{10,9... | collective-permute-start | bytes 3080 | tf_op jit(solution)/shard_map/ppermute | solution.py:15
  67.4 11.5 %collective-permute-start.3 = (s32[256]{0:T(256)S(1)}, s32[256]{0:T(256)S(1)}, u32[]{:S(2)}, u32[]{:S(2)}) collective-permute-start(s32[256]{0:T(256)S(1)} %collective-permute-done.2), channel_id=1, source_target_pairs={{0,1},{1,2},{2,3},{3,4},{4,5},{5,6},{6,7},{7,0},{8,9},{9,10},{10,1... | collective-permute-start | bytes 3080 | tf_op jit(solution)/shard_map/ppermute | solution.py:13
  75.4 4.9 %collective-permute-start.6 = (s32[256]{0:T(256)S(1)}, s32[256]{0:T(256)S(1)}, u32[]{:S(2)}, u32[]{:S(2)}) collective-permute-start(s32[256]{0:T(256)S(1)} %collective-permute-done.5), channel_id=1, source_target_pairs={{0,7},{1,0},{2,1},{3,2},{4,3},{5,4},{6,5},{7,6},{8,15},{9,8},{10,9... | collective-permute-start | bytes 3080 | tf_op jit(solution)/shard_map/ppermute | solution.py:15
  107.5 3.2 %slice-start = ((s8[8388608]{0:T(1024)(128)(4,1)}), s8[4194304]{0:T(1024)(128)(4,1)S(1)}, s32[]{:S(2)}) async-start(s8[8388608]{0:T(1024)(128)(4,1)} %bitcast.39), calls=%async_computation.1 | async-start | bytes 8388608
  108.3 3.1 %slice-start.1 = ((s8[8388608]{0:T(1024)(128)(4,1)}), s8[4194304]{0:T(1024)(128)(4,1)S(1)}, s32[]{:S(2)}) async-start(s8[8388608]{0:T(1024)(128)(4,1)} %bitcast.39), calls=%async_computation.2 | async-start | bytes 8388608
Sparse Core Ops, SparseCore 0:
  101.2 34.4 all-gather.1
